TPU v7x, 256 devices: a whole 4x4x8 slice. The times are simulated.
256 devices in a mesh: ctx: 32 (over z, y), tp: 8 (over x, core).
Axes of the slice: x: 4, y: 4, z: 8, core: 2. Of those that a mesh axis runs over, the one named last changes fastest.
Arguments:
- tokens: bfloat16 [24576, 4096], P(('ctx', 'tp')), may hold values from -6 to 6
- norm_gain: float32 [4096], replicated, may hold values from 0.1 to 1.9
- w_qkv: bfloat16 [4096, 8192], P('ctx', 'tp'), may hold values from -0.09375 to 0.09375
- w_out: bfloat16 [4096, 4096], P('tp', 'ctx'), may hold values from -0.09375 to 0.09375
- head_gain: float32 [4096], P('tp'), may hold values from 0.1 to 1.9
- input_codes: int32 [8, 24576], P('tp', 'ctx'), may hold values from -4 to 4
- forget_codes: int32 [8, 24576], P('tp', 'ctx'), may hold values from -24 to 4
- forget_bias: float32 [8], P('tp'), may hold values from 3 to 13.5, as said below
- document_begin_flags: int32 [24576], P('ctx'), may hold values 0 or 1
Outputs:
- mixed: bfloat16 [24576, 4096], P(('ctx', 'tp'))
Inputs may be any that keep to these rules, and one draw needn't show every extreme that they name: `forget_bias`: a bias for each head.
All inputs are finite; a program needn't handle non-finite values. No bound on the sum of `document_begin_flags` on one device may be relied on, other than what follows from the above.
Results may differ from a plain program's by a relative error of at most 0.017.
Values may be sent and summed in bfloat16 or wider, within the bound.
A program may use at most 64 MiB of HBM per device.

v0:
```python
import jax
import jax.numpy as jnp
from jax import lax
from jax.sharding import PartitionSpec as P

DK = 256
DV = 512
EPSILON = 1e-06
FORGET_STEP = 0.5
INPUT_STEP = 0.5


def carried_in(shard, axis, combine, identity):
    count, position = (lax.axis_size(axis), lax.axis_index(axis))
    everything = jax.tree.map(
        lambda part, kind: lax.all_gather(part.astype(kind), axis),
        shard,
        (jnp.bfloat16, jnp.bfloat16),
    )
    start = jax.tree.map(
        lambda part, zero: jnp.broadcast_to(jnp.asarray(zero, part.dtype), part.shape),
        shard,
        identity,
    )

    def hop(k, before):
        reached = k < position
        new = combine(
            before, jax.tree.map(lambda part, own: part[k].astype(own.dtype), everything, shard)
        )
        return jax.tree.map(lambda a, b: jnp.where(reached, a, b), new, before)

    return lax.fori_loop(0, count, hop, start)


def rms_rows(embedded_entries, norm_gain):
    token_float = embedded_entries.astype(jnp.float32)
    moment = jnp.mean(token_float * token_float, axis=1, keepdims=True)
    return (token_float * lax.rsqrt(moment + EPSILON) * norm_gain).astype(jnp.bfloat16)


def local_terms(queries, key_rows, values, log_forget, input_gate, starts):
    length = queries.shape[0]
    scaling = queries.shape[1] ** (-0.5)
    segment = jnp.cumsum(starts)
    levels = jnp.cumsum(log_forget)
    position = jnp.arange(length)
    allowed = (position[:, None] >= position[None, :]) & (segment[:, None] == segment[None, :])
    decays = jnp.where(
        allowed,
        jnp.exp(jnp.minimum(levels[:, None] - levels[None, :], 0.0) + input_gate[None, :]),
        0.0,
    )
    scores = jnp.dot(queries, key_rows.T, preferred_element_type=jnp.float32) * scaling
    weights = (scores * decays).astype(jnp.bfloat16)
    inner_part = jnp.dot(weights, values, preferred_element_type=jnp.float32)
    last_level = levels[-1]
    last_seg = segment[-1]
    keeping = jnp.where(segment == last_seg, jnp.exp(last_level - levels + input_gate), 0.0)
    weighted = (key_rows.astype(jnp.float32) * keeping[:, None]).astype(jnp.bfloat16)
    local_state = lax.dot_general(
        weighted, values, (((0,), (0,)), ((), ())), preferred_element_type=jnp.float32
    )
    passing = jnp.where(last_seg == 0, jnp.exp(last_level), 0.0)
    carried = jnp.where(segment == 0, jnp.exp(levels), 0.0) * scaling
    return (inner_part, local_state, passing, carried)


def apply_state(queries, carried, incoming):
    lifted = queries.astype(jnp.float32) * carried[:, None]
    return jnp.dot(
        lifted, incoming, precision=lax.Precision.HIGHEST, preferred_element_type=jnp.float32
    )


def head_norm(head_out, gain):
    centre = jnp.mean(head_out, axis=1, keepdims=True)
    shifted = head_out - centre
    spread = jnp.mean(shifted * shifted, axis=1, keepdims=True)
    return (shifted * lax.rsqrt(spread + EPSILON) * gain).astype(jnp.bfloat16)


def combine(earlier, later):
    return (earlier[0] * later[0], later[0][:, None, None] * earlier[1] + later[1])


def local(
    tokens,
    norm_gain,
    w_qkv,
    w_out,
    head_gain,
    input_codes,
    forget_codes,
    forget_bias,
    document_begin_flags,
):
    normed = rms_rows(tokens, norm_gain)
    every_row_list = lax.all_gather(normed, "tp", axis=0, tiled=True)
    parameter_collection = lax.all_gather(w_qkv, "ctx", axis=0, tiled=True)
    rows_combined = jnp.dot(
        every_row_list, parameter_collection, preferred_element_type=jnp.float32
    )
    rows_combined = rows_combined.astype(jnp.bfloat16)
    heads_here = forget_bias.shape[0]
    stride = 2 * DK + DV
    query_list, inner_list, state_list, passing_list, carried_list = ([], [], [], [], [])
    attention_slot_number = 0
    offset = attention_slot_number * stride
    queries = rows_combined[:, offset : offset + DK]
    key_rows = rows_combined[:, offset + DK : offset + 2 * DK]
    values = rows_combined[:, offset + 2 * DK : offset + stride]
    log_forget = jax.nn.log_sigmoid(
        FORGET_STEP * forget_codes[attention_slot_number].astype(jnp.float32)
        + forget_bias[attention_slot_number]
    )
    input_gate = INPUT_STEP * input_codes[attention_slot_number].astype(jnp.float32)
    inner_part, local_state, passing, carried = local_terms(
        queries, key_rows, values, log_forget, input_gate, document_begin_flags
    )
    query_list.append(queries)
    inner_list.append(inner_part)
    state_list.append(local_state)
    passing_list.append(passing)
    carried_list.append(carried)
    identity = (jnp.ones((heads_here,), jnp.float32), jnp.zeros((heads_here, DK, DV), jnp.float32))
    scanned = carried_in((jnp.stack(passing_list), jnp.stack(state_list)), "ctx", combine, identity)
    incoming = scanned[1]
    attention_slot_number = 0
    head_out = inner_list[attention_slot_number] + apply_state(
        query_list[attention_slot_number],
        carried_list[attention_slot_number],
        incoming[attention_slot_number],
    )
    normed_heads = head_norm(head_out, head_gain)
    out_columns = lax.all_gather(w_out, "ctx", axis=1, tiled=True)
    summed = lax.psum_scatter(
        jnp.dot(normed_heads, out_columns, preferred_element_type=jnp.float32).astype(jnp.bfloat16),
        "tp",
        scatter_dimension=0,
        tiled=True,
    ).astype(jnp.float32)
    return (tokens.astype(jnp.float32) + summed).astype(jnp.bfloat16)


def solution(mesh):
    placed = (
        P(("ctx", "tp"), None),
        P(),
        P("ctx", "tp"),
        P("tp", "ctx"),
        P("tp"),
        P("tp", "ctx"),
        P("tp", "ctx"),
        P("tp"),
        P("ctx"),
    )
    return jax.shard_map(
        local, mesh=mesh, in_specs=placed, out_specs=P(("ctx", "tp"), None), check_vma=False
    )
```

profile of v0, /device:TPU:1, one launch (start us, length us, event | category | flops | bytes accessed | tf_op | source)
XLA Modules:
  0.0 411.1 jit_solution(12727475956866767131)
XLA Ops:
  6.5 1.4 fusion.2
  8.0 2.3 fusion.4
  14.2 1.3 exponential_select_fusion
  15.5 42.6 %all-gather.6.cloned.1.call-done = bf16[768,4096]{1,0:T(8,128)(2,1)} async-done(((bf16[96,4096]{1,0:T(8,128)(2,1)}), bf16[768,4096]{1,0:T(8,128)(2,1)}) %all-gather.6.cloned.1.call-update) | async-done | bytes 6291472 | tf_op jit(solution)/shard_map/all_gather | solution.py:99
  58.1 100.4 %all-gather.8.cloned.1.call-done = bf16[4096,1024]{1,0:T(8,128)(2,1)} async-done(((bf16[128,1024]{1,0:T(8,128)(2,1)}), bf16[4096,1024]{1,0:T(8,128)(2,1)}) %all-gather.8.cloned.1.call-update) | async-done | bytes 8388624 | tf_op jit(solution)/shard_map/all_gather | solution.py:100
  158.5 10.9 %convolution_convert_fusion.1 = bf16[768,1024]{1,0:T(8,128)(2,1)S(1)} fusion(bf16[768,4096]{1,0:T(8,128)(2,1)} %all-gather.6.cloned.1.call-done, bf16[4096,1024]{1,0:T(8,128)(2,1)} %all-gather.8.cloned.1.call-done), kind=kOutput, calls=%fused_computation.10 | convolution fusion | flops 6443237376 | bytes 16252928 | tf_op jit(solution)/shard_map/dot_general | solution.py:101
  169.5 1.3 convolution_convert_fusion.2
  174.2 57.4 %all-reduce = bf16[32]{0:T(256)(128)(2,1)S(1)} all-reduce(bf16[32]{0:T(256)(128)(2,1)S(1)} %dynamic-update-slice), channel_id=1, replica_groups=mesh['ctx'=32,'tp'=8] {'ctx'}, use_global_device_ids=true, to_apply=%add | all-reduce | flops 32 | bytes 128
  231.6 2.5 fusion.6
  234.2 32.5 %all-gather.12.cloned.1.call-done = bf16[8192,512]{1,0:T(8,128)(2,1)} async-done(((bf16[256,512]{1,0:T(8,128)(2,1)}), bf16[8192,512]{1,0:T(8,128)(2,1)}) %all-gather.12.cloned.1.call-update) | async-done | bytes 8388624 | tf_op jit(solution)/shard_map/all_gather | solution.py:16
  266.7 81.1 %while.14 = (s32[]{:T(128)}, f32[1,256,512]{2,1,0:T(8,128)S(1)}, s32[]{:T(128)}, bf16[32,1]{0,1:T(2,128)(2,1)S(1)}, bf16[32,1,256,512]{3,2,1,0:T(8,128)(2,1)}, /*index=5*/s32[]{:T(128)}, s32[]{:T(128)}) while((s32[]{:T(128)}, f32[1,256,512]{2,1,0:T(8,128)S(1)}, s32[]{:T(128)}, bf16[32,1]{0,1:T(2,128)(2,1)S(1)}, ...), condition=%wide.region_6.7_spmd.clone, body=%wide.region_5.6_spmd.clone.sunk | while | flops 655365 | bytes 1310839 | solution.py:33
  267.9 1.3 fusion.42
  270.5 1.3 fusion.42
  273.0 1.3 fusion.42
  278.1 1.3 fusion.42
  311.0 1.3 fusion.42
  316.1 1.3 fusion.42
  326.2 1.3 fusion.42
  331.3 1.3 fusion.42
  344.0 1.3 fusion.42
  347.8 3.2 fusion.37
  351.7 7.7 %convolution_convert_fusion = bf16[768,4096]{1,0:T(8,128)(2,1)} fusion(bf16[512,4096]{1,0:T(8,128)(2,1)} %all-gather.10.cloned.1.call-done, f32[768,512]{0,1:T(8,128)S(1)} %get-tuple-element.142, f32[512]{0:T(512)S(1)} %copy-done.5, f32[768]{0:T(1024)S(1)} %add_rsqrt_fusion, f32[768]{0:T(1024)S(1)} %broadcast_multiply_fusion), kind=kOutput, calls=%fused_computation.3 | convolution fusion | flops 3225944064 | bytes 12066816 | tf_op jit(solution)/shard_map/dot_general | solution.py:138
  359.5 42.9 %reduce-scatter.2.cloned.1.call-done = bf16[96,4096]{1,0:T(8,128)(2,1)} async-done(((bf16[768,4096]{1,0:T(8,128)(2,1)}), bf16[96,4096]{1,0:T(8,128)(2,1)}) %reduce-scatter.2.cloned.1.call-update) | async-done | bytes 786448 | tf_op jit(solution)/shard_map/reduce_scatter | solution.py:137
  402.4 2.2 fusion.5
  (102 shorter events, 53.9 us)
Async XLA Ops:
  6.5 5.2 %copy-start.4 = (s32[1,768]{1,0:T(1,128)S(1)}, s32[1,768]{1,0:T(1,128)}, u32[]{:S(2)}) copy-start(s32[1,768]{1,0:T(1,128)} %param.17) | copy-start | bytes 9220
  6.5 5.6 %copy-start.2 = (s32[768]{0:T(1024)S(1)}, s32[768]{0:T(1024)}, u32[]{:S(2)}) copy-start(s32[768]{0:T(1024)} %param.19) | copy-start | bytes 9220
  6.5 51.6 %all-gather.6.cloned.1.call-start = ((), (), s32[]{:S(2)}) async-start(), calls=%async_computation.1 | async-start | bytes 7077888 | tf_op jit(solution)/shard_map/all_gather | solution.py:99
  8.0 6.2 %copy-start.3 = (s32[1,768]{1,0:T(1,128)S(1)}, s32[1,768]{1,0:T(1,128)}, u32[]{:S(2)}) copy-start(s32[1,768]{1,0:T(1,128)} %param.16) | copy-start | bytes 9220
  10.3 148.3 %all-gather.8.cloned.1.call-start = ((), (), s32[]{:S(2)}) async-start(), calls=%async_computation.2 | async-start | bytes 8650752 | tf_op jit(solution)/shard_map/all_gather | solution.py:100
  11.0 255.7 %all-gather.12.cloned.1.call-start = ((), (), s32[]{:S(2)}) async-start(), calls=%async_computation.5 | async-start | bytes 8650752 | tf_op jit(solution)/shard_map/all_gather | solution.py:16
  169.5 64.7 %copy-start.1 = (bf16[768,1024]{1,0:T(8,128)(2,1)}, bf16[768,1024]{1,0:T(8,128)(2,1)S(1)}, u32[]{:S(2)}) copy-start(bf16[768,1024]{1,0:T(8,128)(2,1)S(1)} %convolution_convert_fusion.1) | copy-start | bytes 4718596
  169.5 3.3 copy-start.6
  170.8 180.5 %all-gather.10.cloned.1.call-start = ((), (), s32[]{:S(2)}) async-start(), calls=%async_computation.3 | async-start | bytes 4325376 | tf_op jit(solution)/shard_map/all_gather | solution.py:136
  171.4 231.0 %reduce-scatter.2.cloned.1.call-start = ((), (), s32[]{:S(2)}) async-start(), calls=%async_computation.4 | async-start | bytes 7077888 | tf_op jit(solution)/shard_map/reduce_scatter | solution.py:137
  351.0 0.7 copy-start.5
  359.4 42.9 %copy-start = (bf16[96,4096]{1,0:T(8,128)(2,1)S(1)}, bf16[96,4096]{1,0:T(8,128)(2,1)}, u32[]{:S(2)}) copy-start(bf16[96,4096]{1,0:T(8,128)(2,1)} %param.11) | copy-start | bytes 2359300
Sparse Core Ops, SparseCore 0:
  10.4 47.6 all-gather.5
  60.7 97.8 all-gather.7
  170.9 95.7 all-gather.11
  269.0 77.5 all-gather.9
  359.6 42.7 reduce-scatter.1
where the time goes:
time: 413 us; the launch traced here: 411 us
  waiting for transfers between devices  220 us (53%)
  blocking collectives  57.4 us (14%)
  other arithmetic  48.8 us (12%)
  matrix products  25.7 us (6%)
  local copies, waits for them, and re-layouts  22.3 us (5%)
  loops' own time  21.7 us (5%)
  between operations  15.3 us (4%)
    all_gather x1, waiting for transfers between devices, local(): parameter_collection = lax.all_gather(w_qkv, 'ctx', axis=0, tiled=True)  100 us
    unnamed x1, blocking collectives  57.4 us
    reduce_scatter x1, waiting for transfers between devices, local(): lax.psum_scatter(jnp.dot(normed_heads, out_columns, preferred_element_typ...  42.9 us
    all_gather x1, waiting for transfers between devices, local(): every_row_list = lax.all_gather(normed, 'tp', axis=0, tiled=True)  42.6 us
    select_n x32, other arithmetic, hop(): return jax.tree.map(lambda a, b: jnp.where(reached, a, b), new, before)  40.6 us
    all_gather x1, waiting for transfers between devices, carried_in(): lax.all_gather(part.astype(kind), axis)  32.5 us
    another operation x1, loops' own time, carried_in(): return lax.fori_loop(0, count, hop, start)  21.7 us
    dynamic_slice x32, local copies, waits for them, and re-layouts, hop(): part[k].astype(own.dtype)  18.7 us
  transfers between devices with their start and end apart: 5, of which 4 were waited for; matrix products, arithmetic and copies ran while one was open for 17% of the time, Pallas kernels for 0%

commit v1 on v0

--- a/solution.py
+++ b/solution.py
@@ -8,6 +8,11 @@
 EPSILON = 1e-06
 FORGET_STEP = 0.5
 INPUT_STEP = 0.5
+
+
+def hold_wall(q_in, axis_tag):
+    clean = jnp.concatenate(lax.axis_size(axis_tag) * [q_in], axis=0)
+    return lax.all_to_all(clean, axis_tag, 0, 0, tiled=True)
 
 
 def carried_in(shard, axis, combine, identity):
@@ -97,7 +102,7 @@
 ):
     normed = rms_rows(tokens, norm_gain)
     every_row_list = lax.all_gather(normed, "tp", axis=0, tiled=True)
-    parameter_collection = lax.all_gather(w_qkv, "ctx", axis=0, tiled=True)
+    parameter_collection = hold_wall(w_qkv, "ctx")
     rows_combined = jnp.dot(
         every_row_list, parameter_collection, preferred_element_type=jnp.float32
     )

time: 413 us -> 491 us (1.19)
  waiting for transfers between devices: 220 us -> 260 us
  local copies, waits for them, and re-layouts: 22.3 us -> 40.8 us
  starting transfers between devices: 0.16 us -> 12.5 us
  blocking collectives: 57.4 us -> 66.5 us
    all_to_all x0 -> x1, waiting for transfers between devices: none -> 139 us  [hold_wall(): return lax.all_to_all(clean, axis_tag, 0, 0, tiled=True)]
    all_gather x1 -> x0, waiting for transfers between devices: 100 us -> none  [local(): parameter_collection = lax.all_gather(w_qkv, 'ctx', axis=0, tiled=True)]
    unnamed x17 -> x54, local copies, waits for them, and re-layouts: 1.84 us -> 20.5 us
    all_to_all x0 -> x1, starting transfers between devices: none -> 12.3 us  [hold_wall(): return lax.all_to_all(clean, axis_tag, 0, 0, tiled=True)]
    unnamed x1, blocking collectives: 57.4 us -> 66.5 us
  transfers between devices with their start and end apart: 5 -> 5, of which waited for: 4 -> 4; matrix products, arithmetic and copies ran while one was open for 17% -> 15% of each run, Pallas kernels for 0% -> 0%
where the time goes in v1:
time: 491 us; the launch traced here: 489 us
  waiting for transfers between devices  260 us (53%)
  blocking collectives  66.5 us (14%)
  other arithmetic  46.4 us (9%)
  local copies, waits for them, and re-layouts  40.8 us (8%)
  matrix products  25.7 us (5%)
  loops' own time  21.7 us (4%)
  between operations  15.4 us (3%)
  starting transfers between devices  12.5 us (3%)
    all_to_all x1, waiting for transfers between devices, hold_wall(): return lax.all_to_all(clean, axis_tag, 0, 0, tiled=True)  139 us
    unnamed x1, blocking collectives  66.5 us
    reduce_scatter x1, waiting for transfers between devices, local(): lax.psum_scatter(jnp.dot(normed_heads, out_columns, preferred_element_typ...  43.5 us
    all_gather x1, waiting for transfers between devices, local(): every_row_list = lax.all_gather(normed, 'tp', axis=0, tiled=True)  42.3 us
    select_n x32, other arithmetic, hop(): return jax.tree.map(lambda a, b: jnp.where(reached, a, b), new, before)  40.6 us
    all_gather x1, waiting for transfers between devices, carried_in(): lax.all_gather(part.astype(kind), axis)  33.5 us
    another operation x1, loops' own time, carried_in(): return lax.fori_loop(0, count, hop, start)  21.7 us
    unnamed x54, local copies, waits for them, and re-layouts  20.5 us
  transfers between devices with their start and end apart: 5, of which 4 were waited for; matrix products, arithmetic and copies ran while one was open for 15% of the time, Pallas kernels for 0%

profile of v1, /device:TPU:1, one launch (start us, length us, event | category | flops | bytes accessed | tf_op | source)
XLA Modules:
  0.0 488.6 jit_solution(12271914335880407105)
XLA Ops:
  22.6 3.2 copy-done.1
  25.9 12.3 %all-to-all-start = ((bf16[32,128,1024]{2,1,0:T(8,128)(2,1)}), bf16[32,128,1024]{2,1,0:T(8,128)(2,1)}, u32[]{:S(2)}, u32[]{:S(2)}) async-start(bf16[32,128,1024]{2,1,0:T(8,128)(2,1)} %bitcast.52), calls=%async_computation | async-start | bytes 16777216 | tf_op jit(solution)/shard_map/all_to_all | solution.py:15
  43.9 42.3 %all-gather.5.cloned.1.call-done = bf16[768,4096]{1,0:T(8,128)(2,1)} async-done(((bf16[96,4096]{1,0:T(8,128)(2,1)}), bf16[768,4096]{1,0:T(8,128)(2,1)}) %all-gather.5.cloned.1.call-update) | async-done | bytes 6291472 | tf_op jit(solution)/shard_map/all_gather | solution.py:104
  86.2 139.5 %all-to-all-done = bf16[32,128,1024]{2,1,0:T(8,128)(2,1)} async-done(((bf16[32,128,1024]{2,1,0:T(8,128)(2,1)}), bf16[32,128,1024]{2,1,0:T(8,128)(2,1)}, u32[]{:S(2)}, u32[]{:S(2)}) %all-to-all-start) | async-done | bytes 8388640 | tf_op jit(solution)/shard_map/all_to_all | solution.py:15
  225.7 10.9 %convolution_convert_fusion.1 = bf16[768,1024]{1,0:T(8,128)(2,1)S(1)} fusion(bf16[768,4096]{1,0:T(8,128)(2,1)} %all-gather.5.cloned.1.call-done, bf16[4096,1024]{1,0:T(8,128)(2,1)} %bitcast.1), kind=kOutput, calls=%fused_computation.10 | convolution fusion | flops 6443237376 | bytes 16252928 | tf_op jit(solution)/shard_map/dot_general | solution.py:106
  236.6 1.3 convolution_convert_fusion.2
  241.4 66.5 %all-reduce = bf16[32]{0:T(256)(128)(2,1)S(1)} all-reduce(bf16[32]{0:T(256)(128)(2,1)S(1)} %dynamic-update-slice), channel_id=1, replica_groups=mesh['ctx'=32,'tp'=8] {'ctx'}, use_global_device_ids=true, to_apply=%add | all-reduce | flops 32 | bytes 128
  307.9 2.5 fusion.6
  310.4 33.5 %all-gather.9.cloned.1.call-done = bf16[8192,512]{1,0:T(8,128)(2,1)} async-done(((bf16[256,512]{1,0:T(8,128)(2,1)}), bf16[8192,512]{1,0:T(8,128)(2,1)}) %all-gather.9.cloned.1.call-update) | async-done | bytes 8388624 | tf_op jit(solution)/shard_map/all_gather | solution.py:21
  344.0 81.1 %while.14 = (s32[]{:T(128)}, f32[1,256,512]{2,1,0:T(8,128)S(1)}, s32[]{:T(128)}, bf16[32,1]{0,1:T(2,128)(2,1)S(1)}, bf16[32,1,256,512]{3,2,1,0:T(8,128)(2,1)}, /*index=5*/s32[]{:T(128)}, s32[]{:T(128)}) while((s32[]{:T(128)}, f32[1,256,512]{2,1,0:T(8,128)S(1)}, s32[]{:T(128)}, bf16[32,1]{0,1:T(2,128)(2,1)S(1)}, ...), condition=%wide.region_6.7_spmd.clone, body=%wide.region_5.6_spmd.clone.sunk | while | flops 655365 | bytes 1310839 | solution.py:38
  345.2 1.3 fusion.42
  347.7 1.3 fusion.42
  350.3 1.3 fusion.42
  355.3 1.3 fusion.42
  393.4 1.3 fusion.42
  403.5 1.3 fusion.42
  408.6 1.3 fusion.42
  411.1 1.3 fusion.42
  416.2 1.3 fusion.42
  421.3 1.3 fusion.42
  425.1 3.2 fusion.37
  428.5 7.8 %convolution_convert_fusion = bf16[768,4096]{1,0:T(8,128)(2,1)} fusion(bf16[512,4096]{1,0:T(8,128)(2,1)} %all-gather.7.cloned.1.call-done, f32[768,512]{0,1:T(8,128)S(1)} %get-tuple-element.142, f32[512]{0:T(512)S(1)} %copy-done.8, f32[768]{0:T(1024)S(1)} %add_rsqrt_fusion, f32[768]{0:T(1024)S(1)} %broadcast_multiply_fusion), kind=kOutput, calls=%fused_computation.3 | convolution fusion | flops 3225944064 | bytes 12066816 | tf_op jit(solution)/shard_map/dot_general | solution.py:143
  436.3 43.5 %reduce-scatter.2.cloned.1.call-done = bf16[96,4096]{1,0:T(8,128)(2,1)} async-done(((bf16[768,4096]{1,0:T(8,128)(2,1)}), bf16[96,4096]{1,0:T(8,128)(2,1)}) %reduce-scatter.2.cloned.1.call-update) | async-done | bytes 786448 | tf_op jit(solution)/shard_map/reduce_scatter | solution.py:142
  479.9 2.2 fusion.5
  (139 shorter events, 70.0 us)
Async XLA Ops:
  6.5 15.6 %copy-start = (bf16[128,1024]{1,0:T(8,128)(2,1)S(1)}, bf16[128,1024]{1,0:T(8,128)(2,1)}, u32[]{:S(2)}) copy-start(bf16[128,1024]{1,0:T(8,128)(2,1)} %param.13) | copy-start | bytes 786436
  22.6 3.2 copy-start.1
  25.8 12.4 %copy-start.2 = (bf16[96,4096]{1,0:T(8,128)(2,1)S(1)}, bf16[96,4096]{1,0:T(8,128)(2,1)}, u32[]{:S(2)}) copy-start(bf16[96,4096]{1,0:T(8,128)(2,1)} %param.11) | copy-start | bytes 2359300
  25.8 12.7 %copy-start.4 = (f32[4096]{0:T(1024)S(1)}, f32[4096]{0:T(1024)}, u32[]{:S(2)}) copy-start(f32[4096]{0:T(1024)} %param.12) | copy-start | bytes 49156
  25.8 14.5 %copy-start.7 = (s32[1,768]{1,0:T(1,128)S(1)}, s32[1,768]{1,0:T(1,128)}, u32[]{:S(2)}) copy-start(s32[1,768]{1,0:T(1,128)} %param.17) | copy-start | bytes 9220
  25.8 15.0 %copy-start.5 = (s32[768]{0:T(1024)S(1)}, s32[768]{0:T(1024)}, u32[]{:S(2)}) copy-start(s32[768]{0:T(1024)} %param.19) | copy-start | bytes 9220
  25.8 16.9 %copy-start.6 = (s32[1,768]{1,0:T(1,128)S(1)}, s32[1,768]{1,0:T(1,128)}, u32[]{:S(2)}) copy-start(s32[1,768]{1,0:T(1,128)} %param.16) | copy-start | bytes 9220
  25.9 199.8 %all-to-all-start = ((bf16[32,128,1024]{2,1,0:T(8,128)(2,1)}), bf16[32,128,1024]{2,1,0:T(8,128)(2,1)}, u32[]{:S(2)}, u32[]{:S(2)}) async-start(bf16[32,128,1024]{2,1,0:T(8,128)(2,1)} %bitcast.52), calls=%async_computation | async-start | bytes 16777216 | tf_op jit(solution)/shard_map/all_to_all | solution.py:15
  38.2 48.0 %all-gather.5.cloned.1.call-start = ((), (), s32[]{:S(2)}) async-start(), calls=%async_computation.2 | async-start | bytes 7077888 | tf_op jit(solution)/shard_map/all_gather | solution.py:104
  39.7 304.3 %all-gather.9.cloned.1.call-start = ((), (), s32[]{:S(2)}) async-start(), calls=%async_computation.5 | async-start | bytes 8650752 | tf_op jit(solution)/shard_map/all_gather | solution.py:21
  225.7 14.3 %copy-start.9 = (u32[256]{0:T(256)S(1)}, u32[256]{0:T(256)}, u32[]{:S(2)}) copy-start(u32[256]{0:T(256)} %constant.65) | copy-start | bytes 3076
  236.6 107.3 %copy-start.3 = (bf16[768,1024]{1,0:T(8,128)(2,1)}, bf16[768,1024]{1,0:T(8,128)(2,1)S(1)}, u32[]{:S(2)}) copy-start(bf16[768,1024]{1,0:T(8,128)(2,1)S(1)} %convolution_convert_fusion.1) | copy-start | bytes 4718596
  237.9 190.6 %all-gather.7.cloned.1.call-start = ((), (), s32[]{:S(2)}) async-start(), calls=%async_computation.3 | async-start | bytes 4325376 | tf_op jit(solution)/shard_map/all_gather | solution.py:141
  238.7 241.2 %reduce-scatter.2.cloned.1.call-start = ((), (), s32[]{:S(2)}) async-start(), calls=%async_computation.4 | async-start | bytes 7077888 | tf_op jit(solution)/shard_map/reduce_scatter | solution.py:142
  310.4 118.1 %copy-start.8 = (f32[512]{0:T(512)S(1)}, f32[512]{0:T(512)}, u32[]{:S(2)}) copy-start(f32[512]{0:T(512)} %param.15) | copy-start | bytes 6148
Sparse Core Ops, SparseCore 0:
  40.8 45.3 all-gather.4
  238.1 105.8 all-gather.8
  346.4 77.5 all-gather.6
  436.5 43.3 reduce-scatter.1
